TPU v7x, 32 devices: a whole 2x2x4 slice. The times are simulated.
32 devices in a mesh: dp: 8 (over z, y), mp: 4 (over x, core).
Axes of the slice: x: 2, y: 2, z: 4, core: 2. Of those that a mesh axis runs over, the one named last changes fastest.
Arguments:
- block_input: float32 [4096, 768], P(('dp', 'mp')), may hold values from -54 to 54
- out_cotangent: float32 [4096, 768], P(('dp', 'mp')), may hold values from -6 to 6
- gain_attend: float32 [768], P('dp'), may hold values from 0.5 to 1.5
- weight_triple: float32 [3, 768, 768], P(None, 'dp', 'mp'), may hold values from -4 to 4
- weight_merge: float32 [768, 768], P('mp', 'dp'), may hold values from -0.875 to 0.875
- gain_feed: float32 [768], P('dp'), may hold values from 0.5 to 1.5
- weight_expand: float32 [2, 768, 1152], P(None, 'dp', 'mp'), may hold values from -0.21875 to 0.21875
- weight_reduce: float32 [1152, 768], P('mp', 'dp'), may hold values from -0.1875 to 0.1875
- mean_attend: float32 [768], P('dp'), may hold values from -40 to 40
- mean_triple: float32 [3, 768, 768], P(None, 'dp', 'mp'), may hold values from -40 to 40
- mean_merge: float32 [768, 768], P('mp', 'dp'), may hold values from -40 to 40
- mean_feed: float32 [768], P('dp'), may hold values from -40 to 40
- mean_expand: float32 [2, 768, 1152], P(None, 'dp', 'mp'), may hold values from -40 to 40
- mean_reduce: float32 [1152, 768], P('mp', 'dp'), may hold values from -40 to 40
- square_attend: float32 [768], P('dp'), may hold values from 1.3653333 to 13.653334
- square_triple: float32 [3, 768, 768], P(None, 'dp', 'mp'), may hold values from 1.3653333 to 13.653334
- square_merge: float32 [768, 768], P('mp', 'dp'), may hold values from 1.3653333 to 13.653334
- square_feed: float32 [768], P('dp'), may hold values from 1.3653333 to 13.653334
- square_expand: float32 [2, 768, 1152], P(None, 'dp', 'mp'), may hold values from 1.3653333 to 13.653334
- square_reduce: float32 [1152, 768], P('mp', 'dp'), may hold values from 1.3653333 to 13.653334
Outputs:
- block_output: float32 [4096, 768], P(('dp', 'mp'))
- input_grad: float32 [4096, 768], P(('dp', 'mp'))
- grad_attend: float32 [768], P('dp')
- grad_triple: float32 [3, 768, 768], P(None, 'dp', 'mp')
- grad_merge: float32 [768, 768], P('mp', 'dp')
- grad_feed: float32 [768], P('dp')
- grad_expand: float32 [2, 768, 1152], P(None, 'dp', 'mp')
- grad_reduce: float32 [1152, 768], P('mp', 'dp')
- fresh_attend: float32 [768], P('dp')
- fresh_triple: float32 [3, 768, 768], P(None, 'dp', 'mp')
- fresh_merge: float32 [768, 768], P('mp', 'dp')
- fresh_feed: float32 [768], P('dp')
- fresh_expand: float32 [2, 768, 1152], P(None, 'dp', 'mp')
- fresh_reduce: float32 [1152, 768], P('mp', 'dp')
- first_attend: float32 [768], P('dp')
- first_triple: float32 [3, 768, 768], P(None, 'dp', 'mp')
- first_merge: float32 [768, 768], P('mp', 'dp')
- first_feed: float32 [768], P('dp')
- first_expand: float32 [2, 768, 1152], P(None, 'dp', 'mp')
- first_reduce: float32 [1152, 768], P('mp', 'dp')
- second_attend: float32 [768], P('dp')
- second_triple: float32 [3, 768, 768], P(None, 'dp', 'mp')
- second_merge: float32 [768, 768], P('mp', 'dp')
- second_feed: float32 [768], P('dp')
- second_expand: float32 [2, 768, 1152], P(None, 'dp', 'mp')
- second_reduce: float32 [1152, 768], P('mp', 'dp')
All inputs are finite; a program needn't handle non-finite values.
Results may differ from a plain program's by a relative error of at most 0.017.
Values may be sent and summed in bfloat16 or wider, within the bound.
No kernel may reach another device: no remote copies, remote signals or barrier semaphores. Data moves between devices by JAX's collectives and lax.ppermute only.
A program may use at most 64 MiB of HBM per device.

v0:
```python
import math
import jax
import jax.numpy as jnp
from jax import lax
from jax.sharding import PartitionSpec as P

HD = 64
WINDOW = 128
NORM_EPS = 1e-05
ROPE_BASE = 10000.0
BETA_FIRST = 0.9
BETA_SECOND = 0.999
ADAM_EPS = 1e-08
DECAY = 0.01
RATE_MATRIX = 0.02
RATE_GAIN = 0.2
STEP_COUNT = 3.0
MASKED = -1e30
TILE_ROWS = 128


def normalize(rows_in):
    center = rows_in - jnp.mean(rows_in, axis=-1, keepdims=True)
    scale = lax.rsqrt(jnp.mean(center * center, axis=-1, keepdims=True) + NORM_EPS)
    return (center * scale, scale)


def norm_back(grad_in, normed, scale, gain):
    scaled = grad_in * gain
    return scale * (
        scaled
        - jnp.mean(scaled, axis=-1, keepdims=True)
        - normed * jnp.mean(scaled * normed, axis=-1, keepdims=True)
    )


def rope_tables(length, size):
    half = size // 2
    freqs = jnp.power(jnp.float32(ROPE_BASE), -2.0 * jnp.arange(half, dtype=jnp.float32) / size)
    angles = jnp.arange(length, dtype=jnp.float32)[:, None] * freqs[None, :]
    return (jnp.cos(angles)[:, None, :], jnp.sin(angles)[:, None, :])


def rotate(field, cosine, sine):
    half = field.shape[-1] // 2
    first, second = (field[..., :half], field[..., half:])
    return jnp.concatenate(
        [first * cosine - second * sine, second * cosine + first * sine], axis=-1
    )


def rotate_back(grad, cosine, sine):
    half = grad.shape[-1] // 2
    first, second = (grad[..., :half], grad[..., half:])
    return jnp.concatenate(
        [first * cosine + second * sine, second * cosine - first * sine], axis=-1
    )


def gelu_parts(value):
    normal_share = 0.5 * (1.0 + lax.erf(value * (1.0 / math.sqrt(2.0))))
    density = jnp.exp(-0.5 * value * value) * (1.0 / math.sqrt(2.0 * math.pi))
    return (value * normal_share, normal_share + value * density)


def contract_rows(left, right):
    return lax.dot_general(
        left, right, (((0,), (0,)), ((), ())), preferred_element_type=jnp.float32
    )


def against(left, weight):
    return lax.dot_general(
        left, weight, (((1,), (1,)), ((), ())), preferred_element_type=jnp.float32
    )


def window_mask(start, block, width, length):
    half = (width - block) // 2
    query_pos = start + jnp.arange(block)
    key_pos = start - half + jnp.arange(width)
    near = jnp.abs(query_pos[:, None] - key_pos[None, :]) <= half
    inside = (key_pos >= 0) & (key_pos < length)
    return near & inside[None, :]


def tile_layout(length):
    half = WINDOW // 2
    width = TILE_ROWS + 2 * half
    outer = min(length, 512)
    return (half, width, outer, outer // TILE_ROWS)


def stack_tiles(padded, starts, width):
    return jnp.stack([padded[begin : begin + width] for begin in starts])


def tile_scores(query_tiles, key_tiles, starts, width, length, scale):
    scores = (
        jnp.einsum("bqhd,bkhd->hbqk", query_tiles, key_tiles, preferred_element_type=jnp.float32)
        * scale
    )
    masks = jnp.stack([window_mask(begin, TILE_ROWS, width, length) for begin in starts])
    return jnp.where(masks[None], scores, MASKED)


def attend(query, keys, values):
    length, heads, size = query.shape
    half, width, outer, count = tile_layout(length)
    scale = 1.0 / math.sqrt(size)
    pad_keys = jnp.pad(keys, ((half, half), (0, 0), (0, 0)))
    pad_values = jnp.pad(values, ((half, half), (0, 0), (0, 0)))
    starts = [k * TILE_ROWS for k in range(count)]
    query_tiles = query.reshape(count, TILE_ROWS, heads, size)
    key_tiles = stack_tiles(pad_keys, starts, width)
    value_tiles = stack_tiles(pad_values, starts, width)
    scores = tile_scores(query_tiles, key_tiles, starts, width, length, scale)
    top = jnp.max(scores, axis=-1, keepdims=True)
    total = top + jnp.log(jnp.sum(jnp.exp(scores - top), axis=-1, keepdims=True))
    probs = jnp.exp(scores - total).astype(jnp.bfloat16)
    out_tiles = jnp.einsum(
        "hbqk,bkhd->bqhd", probs, value_tiles, preferred_element_type=jnp.float32
    )
    outputs = out_tiles.reshape(outer, heads, size).astype(jnp.bfloat16)
    totals = total[..., 0].reshape(heads, outer)
    return (outputs, totals)


def attend_back(query, keys, values, attended, totals, d_attended):
    length, heads, size = query.shape
    half, width, outer, count = tile_layout(length)
    scale = 1.0 / math.sqrt(size)
    pad_keys = jnp.pad(keys, ((half, half), (0, 0), (0, 0)))
    pad_values = jnp.pad(values, ((half, half), (0, 0), (0, 0)))
    grad_keys = jnp.zeros((length + 2 * half, heads, size), jnp.float32)
    grad_values = jnp.zeros((length + 2 * half, heads, size), jnp.float32)
    starts = [k * TILE_ROWS for k in range(count)]
    query_tiles = query.reshape(count, TILE_ROWS, heads, size)
    key_tiles = stack_tiles(pad_keys, starts, width)
    value_tiles = stack_tiles(pad_values, starts, width)
    back_tiles = d_attended.reshape(count, TILE_ROWS, heads, size)
    kept_tiles = attended.reshape(count, TILE_ROWS, heads, size)
    scores = tile_scores(query_tiles, key_tiles, starts, width, length, scale)
    lse_tiles = totals.reshape(heads, count, TILE_ROWS)[..., None]
    probs = jnp.exp(scores - lse_tiles)
    probs_b = probs.astype(jnp.bfloat16)
    d_probs = jnp.einsum(
        "bqhd,bkhd->hbqk", back_tiles, value_tiles, preferred_element_type=jnp.float32
    )
    delta = jnp.transpose(
        jnp.sum(back_tiles.astype(jnp.float32) * kept_tiles.astype(jnp.float32), axis=-1), (2, 0, 1)
    )
    d_scores = (probs * (d_probs - delta[..., None]) * scale).astype(jnp.bfloat16)
    grad_query = jnp.einsum(
        "hbqk,bkhd->bqhd", d_scores, key_tiles, preferred_element_type=jnp.float32
    ).reshape(outer, heads, size)
    key_parts = jnp.einsum(
        "hbqk,bqhd->bkhd", d_scores, query_tiles, preferred_element_type=jnp.float32
    )
    value_parts = jnp.einsum(
        "hbqk,bqhd->bkhd", probs_b, back_tiles, preferred_element_type=jnp.float32
    )
    for k in range(count):
        begin = starts[k]
        grad_keys = grad_keys.at[begin : begin + width].add(key_parts[k])
        grad_values = grad_values.at[begin : begin + width].add(value_parts[k])
    return (grad_query, grad_keys[half : half + length], grad_values[half : half + length])


def adam_step(weight, first, second, grad, rate):
    first_new = BETA_FIRST * first + (1.0 - BETA_FIRST) * grad
    second_new = BETA_SECOND * second + (1.0 - BETA_SECOND) * grad * grad
    first_hat = first_new / (1.0 - BETA_FIRST**STEP_COUNT)
    second_hat = second_new / (1.0 - BETA_SECOND**STEP_COUNT)
    fresh = weight - rate * (first_hat / (jnp.sqrt(second_hat) + ADAM_EPS) + DECAY * weight)
    return (fresh, first_new, second_new)


def on_device(
    block_input,
    out_cotangent,
    gain_attend,
    weight_triple,
    weight_merge,
    gain_feed,
    weight_expand,
    weight_reduce,
    mean_attend,
    mean_triple,
    mean_merge,
    mean_feed,
    mean_expand,
    mean_reduce,
    square_attend,
    square_triple,
    square_merge,
    square_feed,
    square_expand,
    square_reduce,
):
    attend_send = (
        gain_attend.astype(jnp.bfloat16),
        weight_triple.astype(jnp.bfloat16),
        weight_merge.astype(jnp.bfloat16),
    )
    feed_send = (
        gain_feed.astype(jnp.bfloat16),
        weight_expand.astype(jnp.bfloat16),
        weight_reduce.astype(jnp.bfloat16),
    )
    gain_one, triple_b, merge_b = (
        lax.all_gather(attend_send[0], "dp", axis=0, tiled=True),
        lax.all_gather(attend_send[1], "dp", axis=1, tiled=True),
        lax.all_gather(attend_send[2], "dp", axis=1, tiled=True),
    )
    gain_one_f = gain_one.astype(jnp.float32)
    normed_one, rstd_one = normalize(block_input)
    hidden_one = (normed_one * gain_one_f).astype(jnp.bfloat16)
    cotangent_b = out_cotangent.astype(jnp.bfloat16)
    hidden_full, cotangent_full = (
        lax.all_gather(hidden_one, "mp", axis=0, tiled=True),
        lax.all_gather(cotangent_b, "mp", axis=0, tiled=True),
    )
    length = hidden_full.shape[0]
    heads = triple_b.shape[2] // HD
    cosine, sine = rope_tables(length, HD)
    pre = jnp.einsum("sd,cdf->csf", hidden_full, triple_b, preferred_element_type=jnp.float32)
    query = rotate(pre[0].reshape(length, heads, HD), cosine, sine).astype(jnp.bfloat16)
    keys = rotate(pre[1].reshape(length, heads, HD), cosine, sine).astype(jnp.bfloat16)
    values = pre[2].reshape(length, heads, HD).astype(jnp.bfloat16)
    attended, totals = attend(query, keys, values)
    attended_flat = attended.reshape(length, heads * HD)
    piece = attended_flat
    residual = block_input + lax.psum_scatter(
        jnp.dot(piece, merge_b, preferred_element_type=jnp.float32),
        "mp",
        scatter_dimension=0,
        tiled=True,
    )
    gain_two, expand_b, reduce_b = (
        lax.all_gather(feed_send[0], "dp", axis=0, tiled=True),
        lax.all_gather(feed_send[1], "dp", axis=1, tiled=True),
        lax.all_gather(feed_send[2], "dp", axis=1, tiled=True),
    )
    gain_two_f = gain_two.astype(jnp.float32)
    normed_two, rstd_two = normalize(residual)
    hidden_two = (normed_two * gain_two_f).astype(jnp.bfloat16)
    second_full = lax.all_gather(hidden_two, "mp", axis=0, tiled=True)
    gate = jnp.dot(second_full, expand_b[0], preferred_element_type=jnp.float32)
    up = jnp.dot(second_full, expand_b[1], preferred_element_type=jnp.float32)
    gelu_value, gelu_slope = gelu_parts(gate)
    inner = (gelu_value * up).astype(jnp.bfloat16)
    piece = inner
    block_output = residual + lax.psum_scatter(
        jnp.dot(piece, reduce_b, preferred_element_type=jnp.float32).astype(jnp.bfloat16),
        "mp",
        scatter_dimension=0,
        tiled=True,
    ).astype(jnp.float32)
    gain_two, expand_b, reduce_b = (
        lax.all_gather(feed_send[0], "dp", axis=0, tiled=True),
        lax.all_gather(feed_send[1], "dp", axis=1, tiled=True),
        lax.all_gather(feed_send[2], "dp", axis=1, tiled=True),
    )
    gain_two_f = gain_two.astype(jnp.float32)
    d_inner = against(cotangent_full, reduce_b)
    d_gate = (d_inner * up * gelu_slope).astype(jnp.bfloat16)
    d_up = (d_inner * gelu_value).astype(jnp.bfloat16)
    reduce_part = contract_rows(inner, cotangent_full)
    expand_part = jnp.stack([contract_rows(second_full, d_gate), contract_rows(second_full, d_up)])
    d_hidden_two = lax.psum_scatter(
        against(d_gate, expand_b[0]) + against(d_up, expand_b[1]),
        "mp",
        scatter_dimension=0,
        tiled=True,
    )
    d_residual = out_cotangent + norm_back(d_hidden_two, normed_two, rstd_two, gain_two_f)
    feed_gain_part = jnp.sum(d_hidden_two * normed_two, axis=0)
    feed_grads = (
        lax.psum_scatter(feed_gain_part, "dp", scatter_dimension=0, tiled=True),
        lax.psum_scatter(expand_part, "dp", scatter_dimension=1, tiled=True),
        lax.psum_scatter(reduce_part, "dp", scatter_dimension=1, tiled=True),
    )
    residual_b = d_residual.astype(jnp.bfloat16)
    residual_full = lax.all_gather(residual_b, "mp", axis=0, tiled=True)
    gain_one, triple_b, merge_b = (
        lax.all_gather(attend_send[0], "dp", axis=0, tiled=True),
        lax.all_gather(attend_send[1], "dp", axis=1, tiled=True),
        lax.all_gather(attend_send[2], "dp", axis=1, tiled=True),
    )
    gain_one_f = gain_one.astype(jnp.float32)
    d_attended = against(residual_full, merge_b).astype(jnp.bfloat16).reshape(length, heads, HD)
    merge_part = contract_rows(attended_flat, residual_full)
    d_query, d_keys, d_values = attend_back(query, keys, values, attended, totals, d_attended)
    d_pre = jnp.stack(
        [rotate_back(d_query, cosine, sine), rotate_back(d_keys, cosine, sine), d_values]
    )
    d_pre = d_pre.astype(jnp.bfloat16).reshape(3, length, heads * HD)
    triple_part = jnp.einsum("sd,csf->cdf", hidden_full, d_pre, preferred_element_type=jnp.float32)
    piece = d_pre
    d_hidden_one = lax.psum_scatter(
        jnp.einsum("csf,cdf->sd", piece, triple_b, preferred_element_type=jnp.float32).astype(
            jnp.bfloat16
        ),
        "mp",
        scatter_dimension=0,
        tiled=True,
    ).astype(jnp.float32)
    input_grad = d_residual + norm_back(d_hidden_one, normed_one, rstd_one, gain_one_f)
    attend_gain_part = jnp.sum(d_hidden_one * normed_one, axis=0)
    attend_grads = (
        lax.psum_scatter(attend_gain_part, "dp", scatter_dimension=0, tiled=True),
        lax.psum_scatter(triple_part, "dp", scatter_dimension=1, tiled=True),
        lax.psum_scatter(merge_part, "dp", scatter_dimension=1, tiled=True),
    )
    grad_attend, grad_feed = lax.psum((attend_grads[0], feed_grads[0]), "mp")
    weights = (gain_attend, weight_triple, weight_merge, gain_feed, weight_expand, weight_reduce)
    grads = (grad_attend, attend_grads[1], attend_grads[2], grad_feed, feed_grads[1], feed_grads[2])
    firsts = (mean_attend, mean_triple, mean_merge, mean_feed, mean_expand, mean_reduce)
    seconds = (
        square_attend,
        square_triple,
        square_merge,
        square_feed,
        square_expand,
        square_reduce,
    )
    rates = (RATE_GAIN, RATE_MATRIX, RATE_MATRIX, RATE_GAIN, RATE_MATRIX, RATE_MATRIX)
    stepped = [
        adam_step(weight, first, second, grad, rate)
        for weight, first, second, grad, rate in zip(weights, firsts, seconds, grads, rates)
    ]
    fresh = tuple((item[0] for item in stepped))
    first_new = tuple((item[1] for item in stepped))
    second_new = tuple((item[2] for item in stepped))
    return (block_output, input_grad) + grads + fresh + first_new + second_new


def solution(mesh):
    in_specs = (
        P(("dp", "mp"), None),
        P(("dp", "mp"), None),
        P("dp"),
        P(None, "dp", "mp"),
        P("mp", "dp"),
        P("dp"),
        P(None, "dp", "mp"),
        P("mp", "dp"),
        P("dp"),
        P(None, "dp", "mp"),
        P("mp", "dp"),
        P("dp"),
        P(None, "dp", "mp"),
        P("mp", "dp"),
        P("dp"),
        P(None, "dp", "mp"),
        P("mp", "dp"),
        P("dp"),
        P(None, "dp", "mp"),
        P("mp", "dp"),
    )
    out_specs = (
        P(("dp", "mp"), None),
        P(("dp", "mp"), None),
        P("dp"),
        P(None, "dp", "mp"),
        P("mp", "dp"),
        P("dp"),
        P(None, "dp", "mp"),
        P("mp", "dp"),
        P("dp"),
        P(None, "dp", "mp"),
        P("mp", "dp"),
        P("dp"),
        P(None, "dp", "mp"),
        P("mp", "dp"),
        P("dp"),
        P(None, "dp", "mp"),
        P("mp", "dp"),
        P("dp"),
        P(None, "dp", "mp"),
        P("mp", "dp"),
        P("dp"),
        P(None, "dp", "mp"),
        P("mp", "dp"),
        P("dp"),
        P(None, "dp", "mp"),
        P("mp", "dp"),
    )
    return jax.shard_map(
        on_device, mesh=mesh, in_specs=in_specs, out_specs=out_specs, check_vma=False
    )
```

profile of v0, /device:TPU:0, one launch (start us, length us, event | category | flops | bytes accessed | tf_op | source)
XLA Modules:
  0.0 576.7 jit_solution(12287532810283591639)
XLA Ops:
  11.0 23.1 %all-reduce.10 = (bf16[768]{0:T(1024)(128)(2,1)S(1)}, bf16[768]{0:T(1024)(128)(2,1)S(1)}) all-reduce(bf16[768]{0:T(1024)(128)(2,1)S(1)} %dynamic-update-slice.24, bf16[768]{0:T(1024)(128)(2,1)S(1)} %dynamic-update-slice.25), channel_id=1, replica_groups=mesh['dp'=8,'mp'=4] {'dp'}, use_global_device_ids=true, to_apply=%add.4 | all-reduce | flops 1536 | bytes 6144
  37.7 9.0 %all_gather.37 = bf16[512,768]{1,0:T(8,128)(2,1)} all-gather(bf16[128,768]{1,0:T(8,128)(2,1)S(1)} %multiply_convert_fusion.4), channel_id=1, replica_groups=mesh['dp'=8,'mp'=4] {'mp'}, dimensions={0}, use_global_device_ids=true | all-gather | bytes 983040 | tf_op jit(solution)/shard_map/all_gather | solution.py:221
  46.9 36.2 %all_gather.38 = bf16[3,768,192]{2,0,1:T(4,128)(2,1)S(1)} all-gather(bf16[3,96,192]{2,0,1:T(4,128)(2,1)S(1)} %copy.152), channel_id=1, replica_groups=mesh['dp'=8,'mp'=4] {'dp'}, dimensions={1}, use_global_device_ids=true | all-gather | bytes 995328 | tf_op jit(solution)/shard_map/all_gather | solution.py:213
  87.2 31.2 %all_gather.39 = bf16[192,768]{0,1:T(8,128)(2,1)S(1)} all-gather(bf16[192,96]{0,1:T(8,128)(2,1)S(1)} %copy.161), channel_id=1, replica_groups=mesh['dp'=8,'mp'=4] {'dp'}, dimensions={1}, use_global_device_ids=true | all-gather | bytes 331776 | tf_op jit(solution)/shard_map/all_gather | solution.py:214
  125.5 31.4 %all_gather.43 = bf16[288,768]{0,1:T(8,128)(2,1)S(1)} all-gather(bf16[288,96]{0,1:T(8,128)(2,1)S(1)} %copy.162), channel_id=1, replica_groups=mesh['dp'=8,'mp'=4] {'dp'}, dimensions={1}, use_global_device_ids=true | all-gather | bytes 497664 | tf_op jit(solution)/shard_map/all_gather | solution.py:243
  157.0 7.6 %all_gather.44 = bf16[512,768]{1,0:T(8,128)(2,1)S(1)} all-gather(bf16[128,768]{1,0:T(8,128)(2,1)S(1)} %convert_element_type.120), channel_id=1, replica_groups=mesh['dp'=8,'mp'=4] {'mp'}, dimensions={0}, use_global_device_ids=true | all-gather | bytes 983040 | tf_op jit(solution)/shard_map/all_gather | solution.py:222
  165.9 33.5 %all_gather.42 = bf16[2,768,288]{2,1,0:T(8,128)(2,1)S(1)} all-gather(bf16[2,96,288]{2,1,0:T(8,128)(2,1)S(1)} %convert_element_type.115), channel_id=1, replica_groups=mesh['dp'=8,'mp'=4] {'dp'}, dimensions={1}, use_global_device_ids=true | all-gather | bytes 995328 | tf_op jit(solution)/shard_map/all_gather | solution.py:242
  200.9 8.6 %all_gather.41 = bf16[512,768]{1,0:T(8,128)(2,1)S(1)} all-gather(bf16[128,768]{1,0:T(8,128)(2,1)S(1)} %multiply_convert_fusion.3), channel_id=1, replica_groups=mesh['dp'=8,'mp'=4] {'mp'}, dimensions={0}, use_global_device_ids=true | all-gather | bytes 983040 | tf_op jit(solution)/shard_map/all_gather | solution.py:248
  215.2 2.5 convolution_convert_fusion
  217.8 2.8 convolution_bitcast_fusion.1
  223.4 3.8 copy.195
  227.2 2.6 reshape.765
  229.9 9.8 %reduce-scatter.21.cloned.1.call-done = f32[128,768]{1,0:T(8,128)} async-done(((f32[512,768]{1,0:T(8,128)}), f32[128,768]{1,0:T(8,128)}) %reduce-scatter.21.cloned.1.call-update) | async-done | bytes 393232 | tf_op jit(solution)/shard_map/reduce_scatter | solution.py:271
  241.5 23.9 %reduce-scatter.19.cloned.1.call-done = bf16[128,768]{1,0:T(8,128)(2,1)} async-done(((bf16[512,768]{1,0:T(8,128)(2,1)}), bf16[128,768]{1,0:T(8,128)(2,1)}) %reduce-scatter.19.cloned.1.call-update) | async-done | bytes 196624 | tf_op jit(solution)/shard_map/reduce_scatter | solution.py:254
  267.4 8.2 %all_gather.45 = bf16[512,768]{1,0:T(8,128)(2,1)S(1)} all-gather(bf16[128,768]{1,0:T(8,128)(2,1)S(1)} %get-tuple-element.256), channel_id=1, replica_groups=mesh['dp'=8,'mp'=4] {'mp'}, dimensions={0}, use_global_device_ids=true | all-gather | bytes 983040 | tf_op jit(solution)/shard_map/all_gather | solution.py:285
  287.3 3.0 copy.191
  290.3 2.8 reshape.761
  296.1 37.4 %reduce-scatter.31.cloned.1.call-done = f32[96,288]{1,0:T(8,128)} async-done(((f32[768,288]{1,0:T(8,128)}), f32[96,288]{1,0:T(8,128)}) %reduce-scatter.31.cloned.1.call-update) | async-done | bytes 110608
  335.3 68.0 %reduce-scatter.29.cloned.1.call-done = f32[96,576]{1,0:T(8,128)} async-done(((f32[768,576]{1,0:T(8,128)}), f32[96,576]{1,0:T(8,128)}) %reduce-scatter.29.cloned.1.call-update) | async-done | bytes 221200
  410.2 58.7 %reduce-scatter.27.cloned.1.call-done = f32[96,192]{1,0:T(8,128)} async-done(((f32[768,192]{1,0:T(8,128)}), f32[96,192]{1,0:T(8,128)}) %reduce-scatter.27.cloned.1.call-update) | async-done | bytes 73744
  470.7 22.9 %reduce-scatter.23.cloned.1.call-done = bf16[128,768]{1,0:T(8,128)(2,1)} async-done(((bf16[512,768]{1,0:T(8,128)(2,1)}), bf16[128,768]{1,0:T(8,128)(2,1)}) %reduce-scatter.23.cloned.1.call-update) | async-done | bytes 196624 | tf_op jit(solution)/shard_map/reduce_scatter | solution.py:301
  494.8 21.8 %all-reduce.8 = (f32[768]{0:T(1024)S(1)}, f32[768]{0:T(1024)S(1)}) all-reduce(f32[768]{0:T(1024)S(1)} %get-tuple-element.228, f32[768]{0:T(1024)S(1)} %copy-done.66), channel_id=6, replica_groups=mesh['dp'=8,'mp'=4] {'dp'}, use_global_device_ids=true, to_apply=%region_16.17.clone | all-reduce | flops 1536 | bytes 12288
  516.7 6.0 %all-reduce.9 = (f32[96]{0:T(128)S(1)}, f32[96]{0:T(128)S(1)}) all-reduce(f32[96]{0:T(128)S(1)} %dynamic-slice.57, f32[96]{0:T(128)S(1)} %dynamic-slice.59), channel_id=1, replica_groups=mesh['dp'=8,'mp'=4] {'mp'}, use_global_device_ids=true, to_apply=%region_17.18 | all-reduce | flops 192 | bytes 1536 | tf_op jit(solution)/shard_map/psum | solution.py:316
  525.8 39.1 %reduce-scatter.25.cloned.1.call-done = f32[96,576]{1,0:T(8,128)} async-done(((f32[768,576]{1,0:T(8,128)}), f32[96,576]{1,0:T(8,128)}) %reduce-scatter.25.cloned.1.call-update) | async-done | bytes 221200
  (312 shorter events, 66.0 us)
Async XLA Ops:
  7.2 192.2 %reduce-scatter.17.cloned.1.call-start = ((), (), s32[]{:S(2)}) async-start(), calls=%async_computation.8 | async-start | bytes 1966080 | tf_op jit(solution)/shard_map/reduce_scatter | solution.py:234
  35.3 47.8 %copy-start.67 = (f32[128]{0:T(128)}, f32[128]{0:T(128)S(1)}, u32[]{:S(2)}) copy-start(f32[128]{0:T(128)S(1)} %broadcast_multiply_fusion.5) | copy-start | bytes 1540
  124.5 115.2 %reduce-scatter.21.cloned.1.call-start = ((), (), s32[]{:S(2)}) async-start(), calls=%async_computation.10 | async-start | bytes 1966080 | tf_op jit(solution)/shard_map/reduce_scatter | solution.py:271
  214.1 51.3 %reduce-scatter.19.cloned.1.call-start = ((), (), s32[]{:S(2)}) async-start(), calls=%async_computation.9 | async-start | bytes 983040 | tf_op jit(solution)/shard_map/reduce_scatter | solution.py:254
  217.7 115.7 %reduce-scatter.31.cloned.1.call-start = ((), (), s32[]{:S(2)}) async-start(), calls=%async_computation.15 | async-start | bytes 1327104
  220.6 182.7 %reduce-scatter.29.cloned.1.call-start = ((), (), s32[]{:S(2)}) async-start(), calls=%async_computation.14 | async-start | bytes 2211840
  229.9 239.0 %reduce-scatter.27.cloned.1.call-start = ((), (), s32[]{:S(2)}) async-start(), calls=%async_computation.13 | async-start | bytes 884736
  282.4 211.2 %reduce-scatter.23.cloned.1.call-start = ((), (), s32[]{:S(2)}) async-start(), calls=%async_computation.11 | async-start | bytes 983040 | tf_op jit(solution)/shard_map/reduce_scatter | solution.py:301
  285.4 279.5 %reduce-scatter.25.cloned.1.call-start = ((), (), s32[]{:S(2)}) async-start(), calls=%async_computation.12 | async-start | bytes 2211840
  334.5 71.9 %copy-start.34 = (f32[288,96]{1,0:T(8,128)}, f32[288,96]{1,0:T(8,128)S(1)}, u32[]{:S(2)}) copy-start(f32[288,96]{1,0:T(8,128)S(1)} %copy.198) | copy-start | bytes 331780
  406.3 63.5 %copy-start.38 = (f32[192,96]{1,0:T(8,128)S(1)}, f32[192,96]{1,0:T(8,128)}, u32[]{:S(2)}) copy-start(f32[192,96]{1,0:T(8,128)} %param.40) | copy-start | bytes 221188
  406.3 63.5 %copy-start.64 = (f32[192,96]{1,0:T(8,128)S(1)}, f32[192,96]{1,0:T(8,128)}, u32[]{:S(2)}) copy-start(f32[192,96]{1,0:T(8,128)} %param.46) | copy-start | bytes 221188
  406.3 63.5 %copy-start.65 = (f32[192,96]{1,0:T(8,128)S(1)}, f32[192,96]{1,0:T(8,128)}, u32[]{:S(2)}) copy-start(f32[192,96]{1,0:T(8,128)} %param.52) | copy-start | bytes 221188
  406.4 87.3 %copy-start.68 = (f32[128]{0:T(128)S(1)}, f32[128]{0:T(128)}, u32[]{:S(2)}) copy-start(f32[128]{0:T(128)} %copy-done.67) | copy-start | bytes 1540
  406.4 87.2 %copy-start.72 = (f32[128]{0:T(128)S(1)}, f32[128]{0:T(128)}, u32[]{:S(2)}) copy-start(f32[128]{0:T(128)} %copy-done.71) | copy-start | bytes 1540
  406.4 88.4 %copy-start.66 = (f32[768]{0:T(1024)S(1)}, f32[768]{0:T(1024)}, u32[]{:S(2)}) copy-start(f32[768]{0:T(1024)} %get-tuple-element.226) | copy-start | bytes 9220
  406.4 116.4 %copy-start.75 = (f32[96]{0:T(128)S(1)}, f32[96]{0:T(128)}, u32[]{:S(2)}) copy-start(f32[96]{0:T(128)} %param.38) | copy-start | bytes 1156
  406.4 116.4 %copy-start.76 = (f32[96]{0:T(128)S(1)}, f32[96]{0:T(128)}, u32[]{:S(2)}) copy-start(f32[96]{0:T(128)} %param.44) | copy-start | bytes 1156
  406.4 116.4 %copy-start.77 = (f32[96]{0:T(128)S(1)}, f32[96]{0:T(128)}, u32[]{:S(2)}) copy-start(f32[96]{0:T(128)} %param.50) | copy-start | bytes 1156
  406.4 116.9 %copy-start.78 = (f32[96]{0:T(128)S(1)}, f32[96]{0:T(128)}, u32[]{:S(2)}) copy-start(f32[96]{0:T(128)} %param.41) | copy-start | bytes 1156
  406.4 116.9 %copy-start.79 = (f32[96]{0:T(128)S(1)}, f32[96]{0:T(128)}, u32[]{:S(2)}) copy-start(f32[96]{0:T(128)} %param.47) | copy-start | bytes 1156
  406.4 116.9 %copy-start.80 = (f32[96]{0:T(128)S(1)}, f32[96]{0:T(128)}, u32[]{:S(2)}) copy-start(f32[96]{0:T(128)} %param.53) | copy-start | bytes 1156
  406.5 117.5 %copy-start.21 = (f32[128,768]{1,0:T(8,128)S(1)}, f32[128,768]{1,0:T(8,128)}, u32[]{:S(2)}) copy-start(f32[128,768]{1,0:T(8,128)} %get-tuple-element.257) | copy-start | bytes 1179652
  469.9 96.1 %copy-start.39 = (f32[192,96]{1,0:T(8,128)}, f32[192,96]{1,0:T(8,128)S(1)}, u32[]{:S(2)}) copy-start(f32[192,96]{1,0:T(8,128)S(1)} %copy.194) | copy-start | bytes 221188
  (67 other events, 590.8 us)
Sparse Core Ops, SparseCore 0:
  124.6 25.7 reduce-scatter.16
  214.3 25.3 reduce-scatter.20
  242.2 23.1 reduce-scatter.18
  268.7 64.6 reduce-scatter.30
  336.8 66.4 reduce-scatter.28
  406.4 62.3 reduce-scatter.26
  471.4 22.1 reduce-scatter.22
  497.1 67.7 reduce-scatter.24
where the time goes:
time: 578 us; the launch traced here: 577 us
  waiting for transfers between devices  260 us (45%)
  blocking collectives  217 us (38%)
  local copies, waits for them, and re-layouts  39.3 us (7%)
  matrix products  22.9 us (4%)
  other arithmetic  20.6 us (4%)
  between operations  16.8 us (3%)
    unnamed x12, waiting for transfers between devices  203 us
    unnamed x2, blocking collectives  44.9 us
    all_gather x1, blocking collectives, on_device(): lax.all_gather(attend_send[1], 'dp', axis=1, tiled=True)  36.2 us
    unnamed x200, local copies, waits for them, and re-layouts  36 us
    all_gather x1, blocking collectives, on_device(): lax.all_gather(feed_send[1], 'dp', axis=1, tiled=True)  33.5 us
    all_gather x1, blocking collectives, on_device(): lax.all_gather(feed_send[2], 'dp', axis=1, tiled=True)  31.4 us
    all_gather x1, blocking collectives, on_device(): lax.all_gather(attend_send[2], 'dp', axis=1, tiled=True)  31.2 us
    reduce_scatter x1, waiting for transfers between devices, on_device(): lax.psum_scatter(jnp.dot(piece, reduce_b, preferred_element_type=jnp.floa...  23.9 us
  transfers between devices with their start and end apart: 8, of which 7 were waited for; matrix products, arithmetic and copies ran while one was open for 9% of the time, Pallas kernels for 0%

commit v1 on v0

--- a/solution.py
+++ b/solution.py
@@ -17,6 +17,18 @@
 STEP_COUNT = 3.0
 MASKED = -1e30
 TILE_ROWS = 128
+
+
+def collect(x, axis, dim):
+    ways, here, step = (lax.axis_size(axis), lax.axis_index(axis), x.shape[dim])
+    line, have = (x, 1)
+    while have < ways:
+        line = jnp.concatenate(
+            [line, lax.ppermute(line, axis, [(d, (d - have) % ways) for d in range(ways)])],
+            axis=dim,
+        )
+        have = 2 * have
+    return jnp.roll(line, here * step, axis=dim)
 
 
 def normalize(rows_in):
@@ -239,7 +251,7 @@
     )
     gain_two, expand_b, reduce_b = (
         lax.all_gather(feed_send[0], "dp", axis=0, tiled=True),
-        lax.all_gather(feed_send[1], "dp", axis=1, tiled=True),
+        collect(feed_send[1], "dp", 1),
         lax.all_gather(feed_send[2], "dp", axis=1, tiled=True),
     )
     gain_two_f = gain_two.astype(jnp.float32)

time: 578 us -> 606 us (1.048)
  blocking collectives: 217 us -> 229 us
  local copies, waits for them, and re-layouts: 39.3 us -> 48.8 us
    all_gather x1, blocking collectives: 31.4 us -> 44.4 us  [on_device(): lax.all_gather(feed_send[2], 'dp', axis=1, tiled=True)]
    unnamed x200 -> x196, local copies, waits for them, and re-layouts: 36 us -> 41.5 us
  transfers between devices with their start and end apart: 8 -> 11, of which waited for: 7 -> 7; matrix products, arithmetic and copies ran while one was open for 9% -> 10% of each run, Pallas kernels for 0% -> 0%
where the time goes in v1:
time: 606 us; the launch traced here: 605 us
  waiting for transfers between devices  262 us (43%)
  blocking collectives  229 us (38%)
  local copies, waits for them, and re-layouts  48.8 us (8%)
  matrix products  24 us (4%)
  other arithmetic  21.1 us (3%)
  between operations  16.9 us (3%)
    unnamed x12, waiting for transfers between devices  203 us
    unnamed x2, blocking collectives  44.9 us
    all_gather x1, blocking collectives, on_device(): lax.all_gather(feed_send[2], 'dp', axis=1, tiled=True)  44.4 us
    unnamed x196, local copies, waits for them, and re-layouts  41.5 us
    all_gather x1, blocking collectives, on_device(): lax.all_gather(attend_send[1], 'dp', axis=1, tiled=True)  36.2 us
    all_gather x1, blocking collectives, on_device(): lax.all_gather(feed_send[1], 'dp', axis=1, tiled=True)  33 us
    all_gather x1, blocking collectives, on_device(): lax.all_gather(attend_send[2], 'dp', axis=1, tiled=True)  31.2 us
    reduce_scatter x1, waiting for transfers between devices, on_device(): lax.psum_scatter(jnp.dot(piece, reduce_b, preferred_element_type=jnp.floa...  23.9 us
  transfers between devices with their start and end apart: 11, of which 7 were waited for; matrix products, arithmetic and copies ran while one was open for 10% of the time, Pallas kernels for 0%

profile of v1, /device:TPU:0, one launch (start us, length us, event | category | flops | bytes accessed | tf_op | source)
XLA Modules:
  0.0 604.6 jit_solution(9427255554667634829)
XLA Ops:
  11.0 23.1 %all-reduce.10 = (bf16[768]{0:T(1024)(128)(2,1)S(1)}, bf16[768]{0:T(1024)(128)(2,1)S(1)}) all-reduce(bf16[768]{0:T(1024)(128)(2,1)S(1)} %dynamic-update-slice.24, bf16[768]{0:T(1024)(128)(2,1)S(1)} %dynamic-update-slice.25), channel_id=1, replica_groups=mesh['dp'=8,'mp'=4] {'dp'}, use_global_device_ids=true, to_apply=%add.4 | all-reduce | flops 1536 | bytes 6144
  37.7 9.0 %all_gather.36 = bf16[512,768]{1,0:T(8,128)(2,1)} all-gather(bf16[128,768]{1,0:T(8,128)(2,1)S(1)} %multiply_convert_fusion.4), channel_id=1, replica_groups=mesh['dp'=8,'mp'=4] {'mp'}, dimensions={0}, use_global_device_ids=true | all-gather | bytes 983040 | tf_op jit(solution)/shard_map/all_gather | solution.py:233
  46.9 36.2 %all_gather.37 = bf16[3,768,192]{2,0,1:T(4,128)(2,1)S(1)} all-gather(bf16[3,96,192]{2,0,1:T(4,128)(2,1)S(1)} %copy.237), channel_id=1, replica_groups=mesh['dp'=8,'mp'=4] {'dp'}, dimensions={1}, use_global_device_ids=true | all-gather | bytes 995328 | tf_op jit(solution)/shard_map/all_gather | solution.py:225
  87.2 31.2 %all_gather.38 = bf16[192,768]{0,1:T(8,128)(2,1)S(1)} all-gather(bf16[192,96]{0,1:T(8,128)(2,1)S(1)} %copy.246), channel_id=1, replica_groups=mesh['dp'=8,'mp'=4] {'dp'}, dimensions={1}, use_global_device_ids=true | all-gather | bytes 331776 | tf_op jit(solution)/shard_map/all_gather | solution.py:226
  127.5 33.0 %all_gather.43 = bf16[2,768,288]{2,0,1:T(2,128)(2,1)S(1)} all-gather(bf16[2,96,288]{2,0,1:T(2,128)(2,1)S(1)} %copy.249), channel_id=1, replica_groups=mesh['dp'=8,'mp'=4] {'dp'}, dimensions={1}, use_global_device_ids=true | all-gather | bytes 995328 | tf_op jit(solution)/shard_map/all_gather | solution.py:274
  165.8 2.6 copy.291
  168.7 7.7 %all_gather.42 = bf16[512,768]{1,0:T(8,128)(2,1)S(1)} all-gather(bf16[128,768]{1,0:T(8,128)(2,1)S(1)} %convert_element_type.120), channel_id=1, replica_groups=mesh['dp'=8,'mp'=4] {'mp'}, dimensions={0}, use_global_device_ids=true | all-gather | bytes 983040 | tf_op jit(solution)/shard_map/all_gather | solution.py:234
  176.7 44.4 %all_gather.41 = bf16[288,768]{0,1:T(8,128)(2,1)S(1)} all-gather(bf16[288,96]{0,1:T(8,128)(2,1)S(1)} %copy.248), channel_id=1, replica_groups=mesh['dp'=8,'mp'=4] {'dp'}, dimensions={1}, use_global_device_ids=true | all-gather | bytes 497664 | tf_op jit(solution)/shard_map/all_gather | solution.py:255
  227.1 8.6 %all_gather.40 = bf16[512,768]{1,0:T(8,128)(2,1)S(1)} all-gather(bf16[128,768]{1,0:T(8,128)(2,1)S(1)} %multiply_convert_fusion.3), channel_id=1, replica_groups=mesh['dp'=8,'mp'=4] {'mp'}, dimensions={0}, use_global_device_ids=true | all-gather | bytes 983040 | tf_op jit(solution)/shard_map/all_gather | solution.py:260
  240.6 2.7 convolution_convert_fusion
  243.3 2.7 convolution_bitcast_fusion.1
  249.3 3.8 copy.284
  255.8 11.5 %reduce-scatter.21.cloned.1.call-done = f32[128,768]{1,0:T(8,128)} async-done(((f32[512,768]{1,0:T(8,128)}), f32[128,768]{1,0:T(8,128)}) %reduce-scatter.21.cloned.1.call-update) | async-done | bytes 393232 | tf_op jit(solution)/shard_map/reduce_scatter | solution.py:283
  269.1 23.9 %reduce-scatter.19.cloned.1.call-done = bf16[128,768]{1,0:T(8,128)(2,1)} async-done(((bf16[512,768]{1,0:T(8,128)(2,1)}), bf16[128,768]{1,0:T(8,128)(2,1)}) %reduce-scatter.19.cloned.1.call-update) | async-done | bytes 196624 | tf_op jit(solution)/shard_map/reduce_scatter | solution.py:266
  295.0 8.2 %all_gather.44 = bf16[512,768]{1,0:T(8,128)(2,1)S(1)} all-gather(bf16[128,768]{1,0:T(8,128)(2,1)S(1)} %get-tuple-element.308), channel_id=1, replica_groups=mesh['dp'=8,'mp'=4] {'mp'}, dimensions={0}, use_global_device_ids=true | all-gather | bytes 983040 | tf_op jit(solution)/shard_map/all_gather | solution.py:297
  315.1 3.0 copy.280
  318.1 2.8 reshape.761
  323.7 37.4 %reduce-scatter.31.cloned.1.call-done = f32[96,288]{1,0:T(8,128)} async-done(((f32[768,288]{1,0:T(8,128)}), f32[96,288]{1,0:T(8,128)}) %reduce-scatter.31.cloned.1.call-update) | async-done | bytes 110608
  363.0 68.0 %reduce-scatter.29.cloned.1.call-done = f32[96,576]{1,0:T(8,128)} async-done(((f32[768,576]{1,0:T(8,128)}), f32[96,576]{1,0:T(8,128)}) %reduce-scatter.29.cloned.1.call-update) | async-done | bytes 221200
  438.0 58.6 %reduce-scatter.27.cloned.1.call-done = f32[96,192]{1,0:T(8,128)} async-done(((f32[768,192]{1,0:T(8,128)}), f32[96,192]{1,0:T(8,128)}) %reduce-scatter.27.cloned.1.call-update) | async-done | bytes 73744
  498.4 23.0 %reduce-scatter.23.cloned.1.call-done = bf16[128,768]{1,0:T(8,128)(2,1)} async-done(((bf16[512,768]{1,0:T(8,128)(2,1)}), bf16[128,768]{1,0:T(8,128)(2,1)}) %reduce-scatter.23.cloned.1.call-update) | async-done | bytes 196624 | tf_op jit(solution)/shard_map/reduce_scatter | solution.py:313
  522.6 21.8 %all-reduce.8 = (f32[768]{0:T(1024)S(1)}, f32[768]{0:T(1024)S(1)}) all-reduce(f32[768]{0:T(1024)S(1)} %get-tuple-element.280, f32[768]{0:T(1024)S(1)} %copy-done.63), channel_id=6, replica_groups=mesh['dp'=8,'mp'=4] {'dp'}, use_global_device_ids=true, to_apply=%region_16.17.clone | all-reduce | flops 1536 | bytes 12288
  544.5 6.0 all-reduce.9
  553.5 39.2 %reduce-scatter.25.cloned.1.call-done = f32[96,576]{1,0:T(8,128)} async-done(((f32[768,576]{1,0:T(8,128)}), f32[96,576]{1,0:T(8,128)}) %reduce-scatter.25.cloned.1.call-update) | async-done | bytes 221200
  (319 shorter events, 79.2 us)
Async XLA Ops:
  7.2 217.5 %reduce-scatter.17.cloned.1.call-start = ((), (), s32[]{:S(2)}) async-start(), calls=%async_computation.8 | async-start | bytes 1966080 | tf_op jit(solution)/shard_map/reduce_scatter | solution.py:246
  125.0 142.3 %reduce-scatter.21.cloned.1.call-start = ((), (), s32[]{:S(2)}) async-start(), calls=%async_computation.10 | async-start | bytes 1966080 | tf_op jit(solution)/shard_map/reduce_scatter | solution.py:283
  125.3 43.2 %collective-permute-start = (bf16[2,96,288]{1,2,0:T(8,128)(2,1)S(1)}, bf16[2,96,288]{1,2,0:T(8,128)(2,1)S(1)}, u32[]{:S(2)}, u32[]{:S(2)}) collective-permute-start(bf16[2,96,288]{1,2,0:T(8,128)(2,1)S(1)} %convert_element_type.115), channel_id=1, source_target_pairs={{0,28},{4,0},{8,4},{12,8},{16,12},{20,16},{24,20},{28,24},{1,29},{... | collective-permute-start | bytes 331784 | tf_op jit(solution)/shard_map/ppermute | solution.py:27
  168.6 7.7 %collective-permute-start.1 = (bf16[2,192,288]{1,2,0:T(8,128)(2,1)S(1)}, bf16[2,192,288]{1,2,0:T(8,128)(2,1)S(1)}, u32[]{:S(2)}, u32[]{:S(2)}) collective-permute-start(bf16[2,192,288]{1,2,0:T(8,128)(2,1)S(1)} %pad_maximum_fusion.5), channel_id=1, source_target_pairs={{0,24},{4,28},{8,0},{12,4},{16,8},{20,12},{24,16},{28,20},{1,25},{... | collective-permute-start | bytes 663560 | tf_op jit(solution)/shard_map/ppermute | solution.py:27
  176.6 45.8 %collective-permute-start.2 = (bf16[2,384,288]{1,2,0:T(8,128)(2,1)S(1)}, bf16[2,384,288]{1,2,0:T(8,128)(2,1)S(1)}, u32[]{:S(2)}, u32[]{:S(2)}) collective-permute-start(bf16[2,384,288]{1,2,0:T(8,128)(2,1)S(1)} %pad_maximum_fusion.2), channel_id=1, source_target_pairs={{0,16},{4,20},{8,24},{12,28},{16,0},{20,4},{24,8},{28,12},{1,17},{... | collective-permute-start | bytes 1327112 | tf_op jit(solution)/shard_map/ppermute | solution.py:27
  240.5 52.5 %reduce-scatter.19.cloned.1.call-start = ((), (), s32[]{:S(2)}) async-start(), calls=%async_computation.9 | async-start | bytes 983040 | tf_op jit(solution)/shard_map/reduce_scatter | solution.py:266
  243.3 117.8 %reduce-scatter.31.cloned.1.call-start = ((), (), s32[]{:S(2)}) async-start(), calls=%async_computation.15 | async-start | bytes 1327104
  246.0 185.0 %reduce-scatter.29.cloned.1.call-start = ((), (), s32[]{:S(2)}) async-start(), calls=%async_computation.14 | async-start | bytes 2211840
  255.7 240.8 %reduce-scatter.27.cloned.1.call-start = ((), (), s32[]{:S(2)}) async-start(), calls=%async_computation.13 | async-start | bytes 884736
  309.9 211.4 %reduce-scatter.23.cloned.1.call-start = ((), (), s32[]{:S(2)}) async-start(), calls=%async_computation.11 | async-start | bytes 983040 | tf_op jit(solution)/shard_map/reduce_scatter | solution.py:313
  313.0 279.8 %reduce-scatter.25.cloned.1.call-start = ((), (), s32[]{:S(2)}) async-start(), calls=%async_computation.12 | async-start | bytes 2211840
  323.0 110.1 %copy-start.11 = (f32[2,96,288]{1,2,0:T(8,128)S(1)}, f32[2,96,288]{1,2,0:T(8,128)}, u32[]{:S(2)}) copy-start(f32[2,96,288]{1,2,0:T(8,128)} %copy-done.10) | copy-start | bytes 663556
  362.2 72.0 %copy-start.30 = (f32[288,96]{1,0:T(8,128)}, f32[288,96]{1,0:T(8,128)S(1)}, u32[]{:S(2)}) copy-start(f32[288,96]{1,0:T(8,128)S(1)} %copy.287) | copy-start | bytes 331780
  434.1 87.2 %copy-start.65 = (f32[128]{0:T(128)S(1)}, f32[128]{0:T(128)}, u32[]{:S(2)}) copy-start(f32[128]{0:T(128)} %copy-done.64) | copy-start | bytes 1540
  434.1 87.2 %copy-start.69 = (f32[128]{0:T(128)S(1)}, f32[128]{0:T(128)}, u32[]{:S(2)}) copy-start(f32[128]{0:T(128)} %copy-done.68) | copy-start | bytes 1540
  434.2 88.4 %copy-start.63 = (f32[768]{0:T(1024)S(1)}, f32[768]{0:T(1024)}, u32[]{:S(2)}) copy-start(f32[768]{0:T(1024)} %get-tuple-element.278) | copy-start | bytes 9220
  434.2 116.4 %copy-start.72 = (f32[96]{0:T(128)S(1)}, f32[96]{0:T(128)}, u32[]{:S(2)}) copy-start(f32[96]{0:T(128)} %param.38) | copy-start | bytes 1156
  434.2 116.4 %copy-start.73 = (f32[96]{0:T(128)S(1)}, f32[96]{0:T(128)}, u32[]{:S(2)}) copy-start(f32[96]{0:T(128)} %param.44) | copy-start | bytes 1156
  434.2 116.4 %copy-start.74 = (f32[96]{0:T(128)S(1)}, f32[96]{0:T(128)}, u32[]{:S(2)}) copy-start(f32[96]{0:T(128)} %param.50) | copy-start | bytes 1156
  434.2 116.9 %copy-start.75 = (f32[96]{0:T(128)S(1)}, f32[96]{0:T(128)}, u32[]{:S(2)}) copy-start(f32[96]{0:T(128)} %param.41) | copy-start | bytes 1156
  434.2 116.9 %copy-start.76 = (f32[96]{0:T(128)S(1)}, f32[96]{0:T(128)}, u32[]{:S(2)}) copy-start(f32[96]{0:T(128)} %param.47) | copy-start | bytes 1156
  434.2 116.9 %copy-start.77 = (f32[96]{0:T(128)S(1)}, f32[96]{0:T(128)}, u32[]{:S(2)}) copy-start(f32[96]{0:T(128)} %param.53) | copy-start | bytes 1156
  434.2 117.5 %copy-start.19 = (f32[128,768]{1,0:T(8,128)S(1)}, f32[128,768]{1,0:T(8,128)}, u32[]{:S(2)}) copy-start(f32[128,768]{1,0:T(8,128)} %get-tuple-element.309) | copy-start | bytes 1179652
  497.6 96.3 %copy-start.35 = (f32[192,96]{1,0:T(8,128)}, f32[192,96]{1,0:T(8,128)S(1)}, u32[]{:S(2)}) copy-start(f32[192,96]{1,0:T(8,128)S(1)} %copy.283) | copy-start | bytes 221188
  (67 other events, 816.1 us)
Sparse Core Ops, SparseCore 0:
  125.1 25.7 reduce-scatter.16
  240.6 26.5 reduce-scatter.20
  269.8 23.1 reduce-scatter.18
  296.3 64.8 reduce-scatter.30
  364.5 66.5 reduce-scatter.28
  434.2 62.3 reduce-scatter.26
  499.1 22.2 reduce-scatter.22
  524.9 67.8 reduce-scatter.24
